TPU v7x, 32 devices: a whole 2x2x4 slice. The times are simulated.
32 devices in a mesh: groups: 2 (over y), seq: 2 (over x), frame: 4 (over z), cfg: 2 (over core).
Axes of the slice: x: 2, y: 2, z: 4, core: 2. Of those that a mesh axis runs over, the one named last changes fastest.
Arguments:
- qkv: bfloat16 [2, 4096, 3, 4096], P('cfg', ('groups', 'frame', 'seq')), parts along dimension 1, may hold values from -108 to 108, as said below
- timestep: int32 [2], P('groups'), parts along dimension 0, may hold values from 0 to 999
- windows: int32 [32], replicated, may hold values from 0 to 2
- segments: int32 [16], P('groups'), parts along dimension 0, may hold values from 0 to 3, never falling along the last dimension, each value on 1 to 4 neighbouring positions
Outputs:
- guided: bfloat16 [4096, 16, 256], P(('groups', 'frame', 'seq'), 'cfg'), parts along dimension 0
There are 2 independent parts, one for each index of `groups`. A program takes and returns all parts, laid end to end along the dimension named above; an argument that names none is the same for every part. Nothing has to cross between parts.
Inputs may be any that keep to these rules, and one draw needn't show every extreme that they name: Entries of qkv lie in this range. `segments`: shot numbers never fall from one frame to the next.
All inputs are finite; a program needn't handle non-finite values.
Results may differ from a plain program's by a relative error of at most 0.0053.
Values may be sent and summed in bfloat16 or wider, within the bound.
A program may use at most 128 MiB of HBM per device.

v0:
```python
import functools
import math

import jax
import jax.numpy as jnp
from jax import lax
from jax.experimental import pallas as pl
from jax.experimental.pallas import tpu as pltpu
from jax.sharding import PartitionSpec as P

HD = 128
W_MAX = 2
NEG = -1e30
LOG2E = 1.4426950408889634
MESH = pl.DeviceIdType.MESH


def gather_kernel(heads_all, levels, room, x_ref, win_ref, out_ref, fits_ref, sem):
    def copy(head, slot):
        return pltpu.make_async_copy(
            x_ref.at[:, :, pl.ds(pl.multiple_of(head * HD, HD), HD)], out_ref.at[slot], sem
        )

    def place(level):
        def step(head, slot):
            hit = win_ref[head] == level

            @pl.when(hit)
            def _():
                copy(head, slot).start()

            return slot + hit.astype(jnp.int32)

        return step

    slot = jnp.int32(0)
    fits = jnp.int32(1)
    for level in range(levels, -1, -1):
        slot = lax.fori_loop(0, heads_all, place(level), slot)
        if level:
            fits = fits * (slot <= room[level - 1]).astype(jnp.int32)
    fits_ref[0] = fits
    pltpu.make_async_copy(out_ref, out_ref, sem).wait()


def kernel(
    dims, x_ref, time_ref, win_ref, seg_ref, out_ref,
    kv, qb, gb, lb, every, rank_ref,
    kv_sem, q_sem, halo_sem, out_sem, a2a_send, own_send, relay_send, out_send, core_send,
    l_sem, l_send,
):
    S, C, F, heads, tl, frames_here, wide, near, short = dims
    groups = S * C
    rows = S * tl
    per_frame = rows // frames_here
    frames = F * frames_here
    s = lax.axis_index("seq")
    c = lax.axis_index("cfg")
    f = lax.axis_index("frame")
    partners = [(ds, dc) for ds in range(S) for dc in range(C) if ds or dc]
    others = [(i, ds, dc) for i, (ds, dc) in enumerate(partners) if ds]
    up_ok = f < F - 1
    down_ok = f > 0

    def at(ds, dc):
        return lax.rem(s + ds, S), lax.rem(c + dc, C)

    def rank(h, s2, c2):
        return h * groups + c2 * S + s2

    def token_rows(base, piece):
        return pl.ds(pl.multiple_of(base + piece * tl, tl), tl)

    def full(core):
        return wide - jnp.where(core > 0, short, 0)

    def shared(core):
        return near - jnp.where(core > 0, short, 0)

    low = near - short

    barrier = pltpu.get_barrier_semaphore()
    for ds, dc in partners:
        s2, c2 = at(ds, dc)
        pl.semaphore_signal(
            barrier, inc=1, device_id={"seq": s2, "cfg": c2}, device_id_type=MESH
        )
    for step in (-1, 1):
        @pl.when((f + step >= 0) & (f + step < F))
        def _():
            for dc in range(C):
                pl.semaphore_signal(
                    barrier, inc=1,
                    device_id={"frame": f + step, "cfg": lax.rem(c + dc, C)},
                    device_id_type=MESH,
                )
    beside = jnp.where(f > 0, C, 0) + jnp.where(f < F - 1, C, 0)
    pl.semaphore_wait(barrier, len(partners) + beside)

    def send_kv(i, ds, dc, h):
        s2, c2 = at(ds, dc)
        return pltpu.make_async_remote_copy(
            src_ref=x_ref.at[rank(h, s2, c2), pl.ds(1, 2)],
            dst_ref=kv.at[h, c, :, token_rows(rows, s), :],
            send_sem=a2a_send.at[0, h, i],
            recv_sem=kv_sem.at[h, s, c],
            device_id={"seq": s2, "cfg": c2}, device_id_type=MESH,
        )

    def send_q(i, ds, dc, h):
        s2, c2 = at(ds, dc)
        return pltpu.make_async_remote_copy(
            src_ref=x_ref.at[rank(h, s2, c2), 0],
            dst_ref=qb.at[h, c, token_rows(0, s), :],
            send_sem=a2a_send.at[1, h, i],
            recv_sem=q_sem.at[h, s, c],
            device_id={"seq": s2, "cfg": c2}, device_id_type=MESH,
        )

    def own_kv(h):
        return pltpu.make_async_copy(
            x_ref.at[rank(h, s, c), pl.ds(1, 2)],
            kv.at[h, c, :, token_rows(rows, s), :],
            kv_sem.at[h, s, c],
        )

    def own_q(h):
        return pltpu.make_async_copy(
            x_ref.at[rank(h, s, c), 0], qb.at[h, c, token_rows(0, s), :], q_sem.at[h, s, c]
        )

    def halo_base(side):
        return 0 if side == 0 else 2 * rows

    def neighbour(side):
        return f + (1 if side == 0 else -1)

    def send_halo(side, dc, h):
        c2 = lax.rem(c + dc, C)
        return pltpu.make_async_remote_copy(
            src_ref=x_ref.at[rank(h, s, c2), pl.ds(1, 2)],
            dst_ref=kv.at[h, c, :, token_rows(halo_base(side), s), :],
            send_sem=own_send.at[side, h, dc],
            recv_sem=halo_sem.at[side, h, s, c],
            device_id={"frame": neighbour(side), "cfg": c2}, device_id_type=MESH,
        )

    def relay(side, i, ds, dc, h):
        s2, b = at(ds, dc)
        return pltpu.make_async_remote_copy(
            src_ref=kv.at[h, b, :, token_rows(rows, s2), :],
            dst_ref=kv.at[h, b, :, token_rows(halo_base(side), s2), :],
            send_sem=relay_send.at[side, h, i],
            recv_sem=halo_sem.at[side, h, s2, b],
            device_id={"frame": neighbour(side)}, device_id_type=MESH,
        )

    def crosses(side, s2, h, core):
        return (h < full(core)) | (s2 == (S - 1 if side == 0 else 0))

    def send_out(ds, h):
        s2 = lax.rem(s + ds, S)
        return pltpu.make_async_remote_copy(
            src_ref=gb.at[h, token_rows(0, s2), :],
            dst_ref=every.at[rank(h, s, c)],
            send_sem=out_send.at[h, ds - 1],
            recv_sem=out_sem.at[rank(h, s, c)],
            device_id={"seq": s2}, device_id_type=MESH,
        )

    def send_core(h, s2, dc, src):
        return pltpu.make_async_remote_copy(
            src_ref=src,
            dst_ref=every.at[rank(h, s2, c)],
            send_sem=core_send.at[h, s2, dc - 1],
            recv_sem=out_sem.at[rank(h, s2, c)],
            device_id={"cfg": lax.rem(c + dc, C)}, device_id_type=MESH,
        )

    def send_local(h, s2, dc):
        c2 = lax.rem(c + dc, C)
        return pltpu.make_async_remote_copy(
            src_ref=x_ref.at[rank(h, s2, c2)],
            dst_ref=lb.at[h - low, s2, c],
            send_sem=l_send.at[h - low, s2, dc],
            recv_sem=l_sem.at[h - low, s2, c],
            device_id={"cfg": c2}, device_id_type=MESH,
        )

    def own_local(h, s2):
        return pltpu.make_async_copy(
            x_ref.at[rank(h, s2, c)], lb.at[h - low, s2, c], l_sem.at[h - low, s2, c]
        )

    def recv(ref, sem):
        pltpu.make_async_remote_copy(
            src_ref=ref, dst_ref=ref, send_sem=sem, recv_sem=sem,
            device_id={"seq": s}, device_id_type=MESH,
        ).wait_recv()

    sides = ((0, up_ok), (1, down_ok))

    def each_partner(h, act):
        for i, (ds, dc) in enumerate(partners):
            @pl.when(h < shared(lax.rem(c + dc, C)))
            def _():
                act(i, ds, dc, h)

    def each_halo(h, act):
        for side, ok in sides:
            for dc in range(C):
                c2 = lax.rem(c + dc, C)

                @pl.when(ok & (h < shared(c2)) & crosses(side, s, h, c2))
                def _():
                    act(send_halo(side, dc, h))

    def each_relay(i, ds, dc, h, act):
        s2, b = at(ds, dc)
        for side, ok in sides:
            @pl.when(ok & crosses(side, s2, h, c))
            def _():
                act(relay(side, i, ds, dc, h))

    def each_local(act):
        @pl.loop(low, heads)
        def _(h):
            for s2 in range(S):
                for dc in range(1, C):
                    @pl.when(h >= shared(lax.rem(c + dc, C)))
                    def _():
                        act(send_local(h, s2, dc))

    @pl.loop(0, near)
    def _(h):
        each_partner(h, lambda *k: send_kv(*k).start())
        each_halo(h, lambda copy: copy.start())

        @pl.when(h < shared(c))
        def _():
            own_kv(h).start()

    each_local(lambda copy: copy.start())

    @pl.loop(shared(c), heads)
    def _(h):
        for s2 in range(S):
            own_local(h, s2).start()

    @pl.loop(0, near)
    def _(h):
        each_partner(h, lambda *k: send_q(*k).start())

        @pl.when(h < shared(c))
        def _():
            own_q(h).start()

    for edge, base in ((f == 0, 0), (f == F - 1, 2 * rows)):
        @pl.when(edge)
        def _():
            @pl.loop(0, near)
            def _(h):
                kv[h, :, :, pl.ds(base, rows), :] = jnp.zeros((C, 2, rows, HD), kv.dtype)

    many = [jnp.int32(0)] * (W_MAX + 1)
    for head in range(heads * groups):
        for level in range(W_MAX + 1):
            many[level] = many[level] + jnp.where(win_ref[head] >= level, 1, 0)
    place = [many[level + 1] if level < W_MAX else jnp.int32(0) for level in range(W_MAX + 1)]
    for head in range(heads * groups):
        mine = place[0]
        for level in range(1, W_MAX + 1):
            mine = jnp.where(win_ref[head] == level, place[level], mine)
        rank_ref[head] = mine
        for level in range(W_MAX + 1):
            place[level] = place[level] + jnp.where(win_ref[head] == level, 1, 0)

    now = jnp.full((1, HD), time_ref[0], jnp.int32).astype(jnp.float32)
    strength = 1.0 + 4.0 * now / 999.0
    factor = LOG2E / math.sqrt(HD)

    def attend(query, keys, values, bias):
        scores = lax.dot_general(
            query, keys, (((1,), (1,)), ((), ())), preferred_element_type=jnp.float32
        )
        if bias is not None:
            scores = scores + bias
        top = jnp.max(scores, axis=1, keepdims=True)
        expd = jnp.exp2((scores - top) * factor)
        total = jnp.sum(expd, axis=1, keepdims=True)
        part = jnp.dot(expd.astype(jnp.bfloat16), values, preferred_element_type=jnp.float32)
        return (part / total).astype(jnp.bfloat16).astype(jnp.float32)

    def guide(cond, uncond):
        return (uncond + strength * (cond - uncond)).astype(jnp.bfloat16)

    @pl.loop(shared(c), heads)
    def _(h):
        for s2 in range(S):
            own_local(h, s2).wait()
            for dc in range(1, C):
                b = lax.rem(c + dc, C)
                recv(lb.at[h - low, s2, b], l_sem.at[h - low, s2, b])
            cond, uncond = [
                attend(lb[h - low, s2, b, 0], lb[h - low, s2, b, 1], lb[h - low, s2, b, 2], None)
                for b in range(C)
            ]
            every[rank(h, s2, c)] = guide(cond, uncond)
            for dc in range(1, C):
                send_core(h, s2, dc, every.at[rank(h, s2, c)]).start()

    @pl.loop(0, shared(c))
    def _(h):
        for i, ds, dc in others:
            s2, b = at(ds, dc)
            recv(kv.at[h, b, :, token_rows(rows, s2), :], kv_sem.at[h, s2, b])
            each_relay(i, ds, dc, h, lambda copy: copy.start())

    def hand_on(h):
        for ds in range(1, S):
            s2 = lax.rem(s + ds, S)
            ref = every.at[rank(h, s2, c)]
            recv(ref, out_sem.at[rank(h, s2, c)])
            for dc in range(1, C):
                send_core(h, s2, dc, ref).start()

    for lo, hi, reach in ((0, full(c), W_MAX), (full(c), shared(c), 1)):
        @pl.loop(lo, hi)
        def _(h):
            own_kv(h).wait()
            own_q(h).wait()
            for ds, dc in partners:
                s2, b = at(ds, dc)
                if not ds:
                    recv(kv.at[h, b, :, token_rows(rows, s2), :], kv_sem.at[h, s2, b])
                recv(qb.at[h, b, token_rows(0, s2), :], q_sem.at[h, s2, b])
            for side, ok in ((0, down_ok), (1, up_ok)):
                for ds in range(S):
                    s2 = lax.rem(s + ds, S)

                    @pl.when(ok & crosses(side, s2, h, c))
                    def _():
                        for b in range(C):
                            recv(
                                kv.at[h, b, :, token_rows(halo_base(side), s2), :],
                                halo_sem.at[side, h, s2, b],
                            )
            me = rank(h, s, c)
            window = jnp.int32(0)
            for level in range(1, W_MAX + 1):
                window = window + jnp.where(me < many[level], 1, 0)
            for number in range(frames_here):
                here = f * frames_here + number
                own_shot = seg_ref[here]
                pieces = []
                for offset in range(-reach, reach + 1):
                    there = here + offset
                    shot = seg_ref[jnp.clip(there, 0, frames - 1)]
                    allowed = (
                        (there >= 0) & (there < frames)
                        & (shot == own_shot) & (abs(offset) <= window)
                    )
                    pieces.append(
                        jnp.full((1, per_frame), jnp.where(allowed, 0.0, NEG), jnp.float32)
                    )
                bias = jnp.concatenate(pieces, axis=1)
                keys = pl.ds((frames_here + number - reach) * per_frame, len(pieces) * per_frame)
                mine = pl.ds(number * per_frame, per_frame)
                cond, uncond = [
                    attend(qb[h, b, mine, :], kv[h, b, 0, keys, :], kv[h, b, 1, keys, :], bias)
                    for b in range(C)
                ]
                gb[h, mine, :] = guide(cond, uncond)
            for ds in range(1, S):
                send_out(ds, h).start()
            for dc in range(1, C):
                send_core(h, s, dc, gb.at[h, token_rows(0, s), :]).start()
            every[me] = gb[h, token_rows(0, s), :]

            @pl.when(h > 0)
            def _():
                hand_on(h - 1)

    hand_on(shared(c) - 1)

    @pl.loop(0, near)
    def _(h):
        each_partner(h, lambda *k: send_kv(*k).wait_send())
        each_partner(h, lambda *k: send_q(*k).wait_send())
        each_halo(h, lambda copy: copy.wait_send())

    @pl.loop(0, shared(c))
    def _(h):
        for i, ds, dc in others:
            each_relay(i, ds, dc, h, lambda copy: copy.wait_send())

    each_local(lambda copy: copy.wait_send())

    @pl.loop(0, heads)
    def _(h):
        for s2 in range(S):
            for dc in range(1, C):
                r = rank(h, s2, lax.rem(c + dc, C))
                recv(every.at[r], out_sem.at[r])

    half = heads
    for s2 in range(S):
        for i in range(half):
            head = s2 * (C * half) + c * half + i
            out_ref[i, :, s2 * HD : (s2 + 1) * HD] = every[rank_ref[head]]

    @pl.loop(0, shared(c))
    def _(h):
        for ds in range(1, S):
            send_out(ds, h).wait_send()

    @pl.loop(0, heads)
    def _(h):
        for s2 in range(S):
            for dc in range(1, C):
                send_core(h, s2, dc, every.at[rank(h, s2, c)]).wait_send()

def body(qkv, timestep, windows, segments):
    S, C, F = (lax.axis_size(axis) for axis in ("seq", "cfg", "frame"))
    x = jnp.transpose(qkv[0], (1, 0, 2))
    tl = x.shape[1]
    heads = x.shape[2] // HD // (S * C)
    frames_here = segments.shape[0] // F
    assert frames_here == W_MAX and heads * S * C * HD == x.shape[2]
    rows = S * tl
    groups = S * C
    n = groups - 1
    dma = pltpu.SemaphoreType.DMA
    wide, near = 3 * heads // 8, 3 * heads // 4
    short = 1 if heads > 4 else 0
    cut = short * S * (C - 1)
    room = (near * groups - cut,) * (W_MAX - 1) + (wide * groups - cut,)
    ordered, fits = pl.pallas_call(
        functools.partial(gather_kernel, heads * groups, W_MAX, room),
        out_shape=(
            jax.ShapeDtypeStruct((heads * groups, 3, tl, HD), x.dtype),
            jax.ShapeDtypeStruct((1,), jnp.int32),
        ),
        in_specs=[pl.BlockSpec(memory_space=pl.ANY), pl.BlockSpec(memory_space=pltpu.SMEM)],
        out_specs=(
            pl.BlockSpec(memory_space=pltpu.VMEM),
            pl.BlockSpec(memory_space=pltpu.SMEM),
        ),
        scratch_shapes=[dma],
        name="order_heads",
        compiler_params=pltpu.CompilerParams(vmem_limit_bytes=56 * 2**20),
    )(x, windows)

    def run(wide, near, short, number):
        kept = max(heads - near + short, 1)

        def call(ordered, timestep, windows, segments):
            return pl.pallas_call(
                functools.partial(kernel, (S, C, F, heads, tl, frames_here, wide, near, short)),
                out_shape=jax.ShapeDtypeStruct((heads, tl, S * HD), jnp.bfloat16),
                in_specs=[pl.BlockSpec(memory_space=pl.ANY)]
                + [pl.BlockSpec(memory_space=pltpu.SMEM)] * 3,
                out_specs=pl.BlockSpec(memory_space=pltpu.VMEM),
                scratch_shapes=[
                    pltpu.VMEM((near, C, 2, 3 * rows, HD), jnp.bfloat16),
                    pltpu.VMEM((near, C, rows, HD), jnp.bfloat16),
                    pltpu.VMEM((near, rows, HD), jnp.bfloat16),
                    pltpu.VMEM((kept, S, C, 3, tl, HD), jnp.bfloat16),
                    pltpu.VMEM((heads * groups, tl, HD), jnp.bfloat16),
                    pltpu.SMEM((heads * groups,), jnp.int32),
                    dma((near, S, C)),
                    dma((near, S, C)),
                    dma((2, near, S, C)),
                    dma((heads * groups,)),
                    dma((2, near, n)),
                    dma((2, near, C)),
                    dma((2, near, n)),
                    dma((near, max(S - 1, 1))),
                    dma((heads, S, C - 1)),
                    dma((kept, S, C)),
                    dma((kept, S, C)),
                ],
                compiler_params=pltpu.CompilerParams(
                    collective_id=number, has_side_effects=True, vmem_limit_bytes=40 * 2**20
                ),
                name=f"guided_attention_{number}",
            )(ordered, timestep, windows, segments)

        return call

    operands = (ordered, timestep, windows, segments)
    if wide and tl * frames_here == rows:
        out = lax.cond(fits[0] > 0, run(wide, near, short, 1), run(heads, heads, 0, 0), *operands)
    else:
        out = run(heads, heads, 0, 0)(*operands)
    return jnp.transpose(out, (1, 0, 2))


def solution(mesh):
    return jax.shard_map(
        body,
        mesh=mesh,
        in_specs=(P("cfg", ("groups", "frame", "seq"), None, None), P("groups"), P(), P("groups")),
        out_specs=P(("groups", "frame", "seq"), "cfg", None),
        check_vma=False,
    )
```

profile of v0, /device:TPU:0, one launch (start us, length us, event | category | flops | bytes accessed | tf_op | source)
XLA Modules:
  0.0 78.1 jit_solution(17652577102022627585)
XLA Ops:
  0.0 0.0 copy-start
  0.0 0.0 copy-start.1
  0.0 4.6 %order_heads.1 = (bf16[32,3,256,128]{3,2,1,0:T(8,128)(2,1)S(1)}, s32[1]{0:T(128)}) custom-call(bf16[3,256,4096]{2,1,0:T(8,128)(2,1)} %bitcast.7, s32[32]{0:T(128)} %win_ref.1), custom_call_target="tpu_custom_call" | custom-call | tf_op jit(solution)/shard_map/order_heads/pallas_call | solution.py:438
  5.3 0.0 copy-done
  5.3 0.0 copy-done.1
  5.3 71.3 %conditional.1 = (bf16[8,256,256]{2,1,0:T(8,128)(2,1)S(1)}) conditional(s32[]{:T(128)} %bitcast.2, (bf16[32,3,256,128]{3,2,1,0:T(8,128)(2,1)S(1)}, s32[1]{0:T(128)}, s32[32]{0:T(128)S(1)}, s32[8]{0:T(128)S(1)}) %tuple.16, (bf16[32,3,256,128]{3,2,1,0:T(8,128)(2,1)S(1)}, s32[1]{0:T(128)}, s32[32]{0:T(128)S(1)}, s32[8]{0:T(128)S(1)}) %tuple.17), branch_computations={%region_0.0_spmd, %region_1.0_spmd} | conditional | bytes 8 | solution.py:493
  5.3 71.2 %guided_attention_1.1 = bf16[8,256,256]{2,1,0:T(8,128)(2,1)S(1)} custom-call(bf16[32,3,256,128]{3,2,1,0:T(8,128)(2,1)S(1)} %get-tuple-element.28.x_ref, s32[1]{0:T(128)} %get-tuple-element.29.time_ref, s32[32]{0:T(128)S(1)} %get-tuple-element.30.win_ref, s32[8]{0:T(128)S(1)} %get-tuple-element.31.seg_ref), custom_call_target="tpu_custom_call" | custom-call | tf_op jit(solution)/shard_map/cond/branch_1_fun/guided_attention_1/pallas_call | solution.py:458
  76.6 1.6 %copy.7 = bf16[8,256,256]{2,0,1:T(8,128)(2,1)} copy(bf16[8,256,256]{2,1,0:T(8,128)(2,1)S(1)} %get-tuple-element.36) | data formatting | bytes 2097152 | tf_op jit(solution)/shard_map/cond | solution.py:493
Async XLA Ops:
  0.0 5.3 %copy-start = (s32[32]{0:T(128)S(1)}, s32[32]{0:T(128)}, u32[]{:S(2)}) copy-start(s32[32]{0:T(128)} %win_ref.1) | copy-start | bytes 388
  0.0 5.3 %copy-start.1 = (s32[8]{0:T(128)S(1)}, s32[8]{0:T(128)}, u32[]{:S(2)}) copy-start(s32[8]{0:T(128)} %param.9) | copy-start | bytes 100
where the time goes:
time: 78.4 us; the launch traced here: 78.1 us
  Pallas kernels  75.9 us (97%)
  local copies, waits for them, and re-layouts  1.56 us (2%)
    pallas_call x1, Pallas kernels, call(): pl.pallas_call(functools.partial(kernel, (S, C, F, heads, tl, frames_here...  71.2 us
    pallas_call x1, Pallas kernels, body(): pl.pallas_call(functools.partial(gather_kernel, heads * groups, W_MAX, ro...  4.63 us

commit v1 on v0

--- a/solution.py
+++ b/solution.py
@@ -13,6 +13,8 @@
 NEG = -1e30
 LOG2E = 1.4426950408889634
 MESH = pl.DeviceIdType.MESH
+KV_EARLY = 2
+KV_EVERY = 4
 
 
 def gather_kernel(heads_all, levels, room, x_ref, win_ref, out_ref, fits_ref, sem):
@@ -420,6 +422,533 @@
             for dc in range(1, C):
                 send_core(h, s2, dc, every.at[rank(h, s2, c)]).wait_send()
 
+
+def plan_kernel(heads_all, levels, room, win_ref, plan_ref, fits_ref):
+    def place(level):
+        def step(head, slot):
+            hit = win_ref[head] == level
+
+            @pl.when(hit)
+            def _():
+                plan_ref[slot] = head
+                plan_ref[heads_all + head] = slot
+
+            return slot + hit.astype(jnp.int32)
+
+        return step
+
+    slot = jnp.int32(0)
+    fits = jnp.int32(1)
+    for level in range(levels, -1, -1):
+        slot = lax.fori_loop(0, heads_all, place(level), slot)
+        if level:
+            plan_ref[2 * heads_all + level - 1] = slot
+            fits = fits * (slot <= room[level - 1]).astype(jnp.int32)
+    fits_ref[0] = fits
+
+
+def fast_kernel(
+    dims, x_ref, plan_ref, time_ref, seg_ref, out_ref,
+    xq, xk, xv, qs, kw, qv, qr, tb, tr, ts, tsr, oh, ohr, hs, hr, ov, ovr, vs, ws, wr, gs, gr, every,
+    la, lr,
+    load_sem, q_send, q_recv, f_send, f_recv, t_send, t_recv, k_send, k_recv, s_send, s_recv,
+    c_send, c_recv, w_send, w_recv, g_send, g_recv, h_send, h_recv, e_send, e_recv,
+    l_send, l_recv,
+):
+    F, heads_all, W, M, tl = dims
+    N = M - W
+    L = heads_all - M
+    s = lax.axis_index("seq")
+    c = lax.axis_index("cfg")
+    f = lax.axis_index("frame")
+    frames = 2 * F
+    dz = 1 - 2 * s
+    up_ok, down_ok = f < F - 1, f > 0
+    fwd, back = f + dz, f - dz
+    fwd_ok = (fwd >= 0) & (fwd < F)
+    back_ok = (back >= 0) & (back < F)
+    lanes = [slice(128 * j, 128 * (j + 1)) for j in range(tl // 128)]
+    k = len(lanes)
+
+    own = (xq, xk, xv)
+    for part, ref in enumerate(own):
+        @pl.loop(0, heads_all)
+        def _(h):
+            pltpu.make_async_copy(
+                x_ref.at[part, :, pl.ds(pl.multiple_of(h * HD, HD), HD)], ref.at[h],
+                load_sem.at[part],
+            ).start()
+
+    def loaded(part):
+        pltpu.make_async_copy(own[part], own[part], load_sem.at[part]).wait()
+
+    barrier = pltpu.get_barrier_semaphore()
+    for axis, other in (("seq", 1 - s), ("cfg", 1 - c)):
+        pl.semaphore_signal(barrier, inc=1, device_id={axis: other}, device_id_type=MESH)
+    for ok, step in ((up_ok, 1), (down_ok, -1)):
+        @pl.when(ok)
+        def _():
+            pl.semaphore_signal(
+                barrier, inc=1, device_id={"frame": f + step}, device_id_type=MESH
+            )
+
+    def remote(src, dst, send, arrive, where):
+        return pltpu.make_async_remote_copy(
+            src_ref=src, dst_ref=dst, send_sem=send, recv_sem=arrive,
+            device_id=where, device_id_type=MESH,
+        )
+
+    across = {"seq": 1 - s}
+    beside = {"cfg": 1 - c}
+
+    def send_q(i):
+        return remote(qs.at[i], qv.at[i], q_send.at[i], q_recv.at[i], across)
+
+    def send_fwd(n):
+        return remote(qv.at[W + n], qr.at[n], f_send.at[n], f_recv.at[n], {"frame": fwd})
+
+    def send_third(n):
+        return (
+            remote(tb.at[n], tr.at[n], t_send.at[0, n], t_recv.at[0, n], {"frame": back}),
+            remote(ts.at[n], tsr.at[n], t_send.at[1, n], t_recv.at[1, n], {"frame": back}),
+        )
+
+    def send_kv(side, i):
+        start = 0 if side == 0 else 2 * tl
+        return remote(
+            kw.at[i, :, pl.ds(tl, tl), :], kw.at[i, :, pl.ds(start, tl), :],
+            k_send.at[side, i], k_recv.at[side, i], {"frame": f + 1 if side == 0 else f - 1},
+        )
+
+    def send_stats(i):
+        return remote(hs.at[i], hr.at[i], s_send.at[i], s_recv.at[i], across)
+
+    def send_near_stats():
+        part = pl.ds(W, N)
+        return remote(hs.at[part], hr.at[part], s_send.at[W], s_recv.at[W], across)
+
+    def send_part(i):
+        return remote(ov.at[i], ovr.at[i], c_send.at[i], c_recv.at[i], beside)
+
+    def send_weight(i):
+        return remote(ws.at[i], wr.at[i], w_send.at[i], w_recv.at[i], across)
+
+    def send_guided(i):
+        return remote(gs.at[i], gr.at[i], g_send.at[i], g_recv.at[i], across)
+
+    def send_home(i):
+        return remote(oh.at[i], ohr.at[i], h_send.at[i], h_recv.at[i], beside)
+
+    def send_final(i):
+        return remote(every.at[i], every.at[i], e_send.at[i], e_recv.at[i], beside)
+
+    def send_local(n):
+        return remote(la.at[n], lr.at[n], l_send.at[n], l_recv.at[n], beside)
+
+    def mine(i):
+        return lax.rem(i, 2) == c
+
+    factor = LOG2E / math.sqrt(HD)
+    rows_id = lax.broadcasted_iota(jnp.int32, (128, 128), 0)
+    lanes_id = lax.broadcasted_iota(jnp.int32, (128, 128), 1)
+    eye = rows_id == lanes_id
+    now = jnp.full((1, HD), time_ref[0], jnp.int32).astype(jnp.float32)
+    strength = 1.0 + 4.0 * now / 999.0
+    coef = jnp.where(c == 0, strength, 1.0 - strength)
+
+    def to_row(column):
+        return [
+            jnp.sum(jnp.where(eye, column[part], 0.0), axis=0, keepdims=True) for part in lanes
+        ]
+
+    def to_column(row):
+        return jnp.concatenate(
+            [
+                jnp.sum(jnp.where(eye, row[j : j + 1], 0.0), axis=1, keepdims=True)
+                for j in range(k)
+            ],
+            axis=0,
+        )
+
+    def attend(query, keys, values, bias=None):
+        scores = lax.dot_general(
+            query, keys, (((1,), (1,)), ((), ())), preferred_element_type=jnp.float32
+        )
+        if bias is not None:
+            scores = scores + bias
+        top = jnp.max(scores, axis=1, keepdims=True)
+        expd = jnp.exp2((scores - top) * factor)
+        total = jnp.sum(expd, axis=1, keepdims=True)
+        part = jnp.dot(expd.astype(jnp.bfloat16), values, preferred_element_type=jnp.float32)
+        return part / total, top, total
+
+    def keep_stats(ref, i, top, total):
+        for j, row in enumerate(to_row(top) + to_row(total)):
+            ref[i, j : j + 1, :] = row
+
+    me = 2 * f + s
+    visitor = 2 * f + 1 - s
+    beyond = me + 2 * dz
+
+    def shot(frame):
+        return seg_ref[jnp.clip(frame, 0, frames - 1)]
+
+    same_visit = shot(me) == shot(visitor)
+    same_beyond = fwd_ok & (shot(visitor) == shot(beyond))
+    same_low = down_ok & (shot(me) == shot(me - 2))
+    same_high = up_ok & (shot(me) == shot(me + 2))
+
+    def reach(level, i):
+        return i < plan_ref[2 * heads_all + level - 1]
+
+    def piece(allowed):
+        return jnp.full((1, tl), jnp.where(allowed, 0.0, NEG), jnp.float32)
+
+    loaded(0)
+
+    @pl.loop(0, M)
+    def _(i):
+        qs[i] = xq[plan_ref[i]]
+
+    pl.semaphore_wait(
+        barrier, 2 + jnp.where(up_ok, 1, 0) + jnp.where(down_ok, 1, 0)
+    )
+
+    @pl.loop(W, M)
+    def _(i):
+        send_q(i).start()
+
+    loaded(1)
+    loaded(2)
+
+    @pl.loop(0, W)
+    def _(i):
+        for part in range(2):
+            kw[i, part, pl.ds(tl, tl), :] = own[1 + part][plan_ref[i]]
+
+    def spread_kv(i):
+        for side, ok in ((0, up_ok), (1, down_ok)):
+            @pl.when(ok)
+            def _():
+                send_kv(side, i).start()
+
+    EARLY = min(W, KV_EARLY)
+    for i in range(EARLY):
+        spread_kv(i)
+
+    for ok, start in ((down_ok, 0), (up_ok, 2 * tl)):
+        @pl.when(jnp.logical_not(ok))
+        def _():
+            @pl.loop(0, W)
+            def _(i):
+                kw[i, :, pl.ds(start, tl), :] = jnp.zeros((2, tl, HD), kw.dtype)
+
+    @pl.when(jnp.logical_not(fwd_ok))
+    def _():
+        @pl.loop(0, N)
+        def _(n):
+            tr[n] = jnp.zeros((tl, HD), tr.dtype)
+            tsr[n] = jnp.zeros((2 * k, 128), tsr.dtype)
+
+    @pl.loop(W, M)
+    def _(i):
+        here = plan_ref[i]
+        out, top, total = attend(qs[i], xk[here], xv[here])
+        oh[i] = out
+        keep_stats(hs, i, top, total)
+
+    send_near_stats().start()
+
+    @pl.loop(0, W)
+    def _(i):
+        send_q(i).start()
+
+    LAG = 2
+
+    @pl.loop(0, max(N + LAG, L))
+    def _(n):
+        @pl.when(n < N)
+        def _():
+            i = W + n
+            send_q(i).wait_recv()
+
+            @pl.when(fwd_ok)
+            def _():
+                send_fwd(n).start()
+
+            here = plan_ref[i]
+            out, top, total = attend(qv[i], xk[here], xv[here])
+            ov[i] = out
+            keep_stats(vs, i, top, total)
+
+        @pl.when((n >= LAG) & (n < N + LAG) & back_ok)
+        def _():
+            m = n - LAG
+            send_fwd(m).wait_recv()
+            here = plan_ref[W + m]
+            out, top, total = attend(qr[m], xk[here], xv[here])
+            tb[m] = out.astype(jnp.bfloat16)
+            keep_stats(ts, m, top, total)
+            for copy in send_third(m):
+                copy.start()
+
+        late = EARLY + n // KV_EVERY
+
+        @pl.when((lax.rem(n, KV_EVERY) == KV_EVERY - 1) & (late < W))
+        def _():
+            spread_kv(late)
+
+        @pl.when(n < L)
+        def _():
+            here = plan_ref[M + n]
+            out, _, _ = attend(xq[here], xk[here], xv[here])
+            la[n] = out.astype(jnp.bfloat16)
+            send_local(n).start()
+
+    spread = min(W, EARLY + max(N + LAG, L) // KV_EVERY)
+
+    @pl.loop(spread, W)
+    def _(i):
+        spread_kv(i)
+
+    def weigh(i, home, parts):
+        tops = [
+            ref[at, 0:k, :] + jnp.full((1, 128), jnp.where(ok, 0.0, NEG), jnp.float32)
+            for ref, at, ok in parts
+        ]
+        tops.append(home[i, 0:k, :])
+        high = functools.reduce(jnp.maximum, tops)
+        sums = [ref[at, k : 2 * k, :] for ref, at, _ in parts] + [home[i, k : 2 * k, :]]
+        mass = [jnp.exp2((top - high) * factor) * total for top, total in zip(tops, sums)]
+        whole = sum(mass)
+        shares = [part / whole for part in mass]
+        ws[i] = shares[-1]
+        send_weight(i).start()
+        return [to_column(share) * coef for share in shares[:-1]]
+
+    def hand_over(i):
+        @pl.when(jnp.logical_not(mine(i)))
+        def _():
+            send_part(i).start()
+
+    def join(i):
+        @pl.when(mine(i))
+        def _():
+            send_part(i).wait_recv()
+            gs[i] = (ov[i] + ovr[i]).astype(jnp.bfloat16)
+            send_guided(i).start()
+
+    def weigh_home(i):
+        send_weight(i).wait_recv()
+        oh[i] = oh[i] * (to_column(wr[i]) * coef)
+
+        @pl.when(jnp.logical_not(mine(i)))
+        def _():
+            send_home(i).start()
+
+    def finish(i):
+        @pl.when(mine(i))
+        def _():
+            send_home(i).wait_recv()
+            send_guided(i).wait_recv()
+            every[i] = (gr[i].astype(jnp.float32) + oh[i] + ohr[i]).astype(jnp.bfloat16)
+            send_final(i).start()
+
+    send_near_stats().wait_recv()
+
+    @pl.loop(0, N)
+    def _(n):
+        i = W + n
+
+        @pl.when(fwd_ok)
+        def _():
+            for copy in send_third(n):
+                copy.wait_recv()
+
+        near = reach(1, i)
+        first, second = weigh(
+            i, hr, [(vs, i, near & same_visit), (tsr, n, near & same_beyond)]
+        )
+        ov[i] = first * ov[i] + second * tr[n].astype(jnp.float32)
+        hand_over(i)
+
+    @pl.loop(0, L)
+    def _(n):
+        send_local(n).wait_recv()
+        here, there = la[n].astype(jnp.float32), lr[n].astype(jnp.float32)
+        cond = jnp.where(c == 0, here, there)
+        uncond = jnp.where(c == 0, there, here)
+        every[M + n] = (uncond + strength * (cond - uncond)).astype(jnp.bfloat16)
+
+    first_keys = pl.multiple_of(tl * (1 - s), tl)
+    per = -(-N // W)
+
+    @pl.loop(0, W + 4)
+    def _(j):
+        @pl.when(j < W)
+        def _():
+            send_q(j).wait_recv()
+
+            @pl.when(down_ok)
+            def _():
+                send_kv(0, j).wait_recv()
+
+            @pl.when(up_ok)
+            def _():
+                send_kv(1, j).wait_recv()
+
+            wide = reach(2, j)
+            near = reach(1, j)
+            bias = jnp.concatenate(
+                [piece(wide & same_low), piece(True), piece(wide & same_high)], axis=1
+            )
+            out, top, total = attend(qs[j], kw[j, 0], kw[j, 1], bias)
+            oh[j] = out
+            keep_stats(hs, j, top, total)
+            send_stats(j).start()
+            one = near & same_visit
+            two = near & same_beyond
+            bias = jnp.concatenate(
+                [
+                    piece(jnp.where(s == 0, one, two)),
+                    piece(jnp.where(s == 0, two, one)),
+                ],
+                axis=1,
+            )
+            keys = pl.ds(first_keys, 2 * tl)
+            out, top, total = attend(qv[j], kw[j, 0, keys, :], kw[j, 1, keys, :], bias)
+            ov[j] = out
+            keep_stats(vs, j, top, total)
+
+        @pl.when((j >= 2) & (j < W + 2))
+        def _():
+            m = j - 2
+            send_stats(m).wait_recv()
+            (share,) = weigh(m, hr, [(vs, m, reach(1, m) & (same_visit | same_beyond))])
+            ov[m] = share * ov[m]
+            hand_over(m)
+
+        for part in range(per):
+            n = per * j + part
+
+            @pl.when(n < N)
+            def _():
+                join(W + n)
+
+            late = per * (j - 3) + part
+
+            @pl.when((late >= 0) & (late < N))
+            def _():
+                weigh_home(W + late)
+
+        @pl.when((j >= 2) & (j < W + 2))
+        def _():
+            join(j - 2)
+
+        @pl.when(j >= 4)
+        def _():
+            weigh_home(j - 4)
+
+        for part in range(per):
+            late = per * (j - 3) + part
+
+            @pl.when((late >= 0) & (late < N))
+            def _():
+                finish(W + late)
+
+        @pl.when(j >= 4)
+        def _():
+            finish(j - 4)
+
+    @pl.loop(0, M)
+    def _(i):
+        @pl.when(jnp.logical_not(mine(i)))
+        def _():
+            send_final(i).wait_recv()
+
+    half = heads_all // 4
+    for s2 in range(2):
+        for i in range(half):
+            head = s2 * (2 * half) + c * half + i
+            out_ref[i, :, s2 * HD : (s2 + 1) * HD] = every[plan_ref[heads_all + head]]
+
+    @pl.loop(0, M)
+    def _(i):
+        send_q(i).wait_send()
+        send_weight(i).wait_send()
+
+        @pl.when(mine(i))
+        def _():
+            send_guided(i).wait_send()
+            send_final(i).wait_send()
+
+        @pl.when(jnp.logical_not(mine(i)))
+        def _():
+            send_part(i).wait_send()
+            send_home(i).wait_send()
+
+    @pl.loop(0, N)
+    def _(n):
+        @pl.when(fwd_ok)
+        def _():
+            send_fwd(n).wait_send()
+
+        @pl.when(back_ok)
+        def _():
+            for copy in send_third(n):
+                copy.wait_send()
+
+    send_near_stats().wait_send()
+
+    @pl.loop(0, W)
+    def _(i):
+        send_stats(i).wait_send()
+        for side, ok in ((0, up_ok), (1, down_ok)):
+            @pl.when(ok)
+            def _():
+                send_kv(side, i).wait_send()
+
+    @pl.loop(0, L)
+    def _(n):
+        send_local(n).wait_send()
+
+
+def fast_call(F, heads_all, W, M, tl, number):
+    N, L, k = M - W, heads_all - M, tl // 128
+    dma = pltpu.SemaphoreType.DMA
+
+    def block(count, dtype=jnp.bfloat16):
+        return pltpu.VMEM((count, tl, HD), dtype)
+
+    def small(count, rows):
+        return pltpu.VMEM((count, rows, 128), jnp.float32)
+
+    f32 = jnp.float32
+    return pl.pallas_call(
+        functools.partial(fast_kernel, (F, heads_all, W, M, tl)),
+        out_shape=jax.ShapeDtypeStruct((heads_all // 4, tl, 2 * HD), jnp.bfloat16),
+        in_specs=[pl.BlockSpec(memory_space=pl.ANY)]
+        + [pl.BlockSpec(memory_space=pltpu.SMEM)] * 3,
+        out_specs=pl.BlockSpec(memory_space=pltpu.VMEM),
+        scratch_shapes=[
+            block(heads_all), block(heads_all), block(heads_all),
+            block(M), pltpu.VMEM((W, 2, 3 * tl, HD), jnp.bfloat16), block(M),
+            block(N), block(N), block(N), small(N, 2 * k), small(N, 2 * k),
+            block(M, f32), block(M, f32), small(M, 2 * k), small(M, 2 * k),
+            block(M, f32), block(M, f32), small(M, 2 * k), small(M, k), small(M, k),
+            block(M), block(M), block(heads_all), block(L), block(L),
+            dma((3,)), dma((M,)), dma((M,)), dma((N,)), dma((N,)), dma((2, N)), dma((2, N)),
+            dma((2, W)), dma((2, W)), dma((W + 1,)), dma((W + 1,)),
+            dma((M,)), dma((M,)), dma((M,)), dma((M,)), dma((M,)), dma((M,)),
+            dma((M,)), dma((M,)), dma((M,)), dma((M,)), dma((L,)), dma((L,)),
+        ],
+        compiler_params=pltpu.CompilerParams(
+            collective_id=number, has_side_effects=True, vmem_limit_bytes=56 * 2**20
+        ),
+        name=f"visiting_attention_{number}",
+    )
+
+
 def body(qkv, timestep, windows, segments):
     S, C, F = (lax.axis_size(axis) for axis in ("seq", "cfg", "frame"))
     x = jnp.transpose(qkv[0], (1, 0, 2))
@@ -431,68 +960,78 @@
     groups = S * C
     n = groups - 1
     dma = pltpu.SemaphoreType.DMA
-    wide, near = 3 * heads // 8, 3 * heads // 4
-    short = 1 if heads > 4 else 0
-    cut = short * S * (C - 1)
-    room = (near * groups - cut,) * (W_MAX - 1) + (wide * groups - cut,)
-    ordered, fits = pl.pallas_call(
-        functools.partial(gather_kernel, heads * groups, W_MAX, room),
-        out_shape=(
-            jax.ShapeDtypeStruct((heads * groups, 3, tl, HD), x.dtype),
-            jax.ShapeDtypeStruct((1,), jnp.int32),
-        ),
-        in_specs=[pl.BlockSpec(memory_space=pl.ANY), pl.BlockSpec(memory_space=pltpu.SMEM)],
-        out_specs=(
-            pl.BlockSpec(memory_space=pltpu.VMEM),
-            pl.BlockSpec(memory_space=pltpu.SMEM),
-        ),
-        scratch_shapes=[dma],
-        name="order_heads",
-        compiler_params=pltpu.CompilerParams(vmem_limit_bytes=56 * 2**20),
-    )(x, windows)
-
-    def run(wide, near, short, number):
-        kept = max(heads - near + short, 1)
-
-        def call(ordered, timestep, windows, segments):
-            return pl.pallas_call(
-                functools.partial(kernel, (S, C, F, heads, tl, frames_here, wide, near, short)),
-                out_shape=jax.ShapeDtypeStruct((heads, tl, S * HD), jnp.bfloat16),
-                in_specs=[pl.BlockSpec(memory_space=pl.ANY)]
-                + [pl.BlockSpec(memory_space=pltpu.SMEM)] * 3,
-                out_specs=pl.BlockSpec(memory_space=pltpu.VMEM),
-                scratch_shapes=[
-                    pltpu.VMEM((near, C, 2, 3 * rows, HD), jnp.bfloat16),
-                    pltpu.VMEM((near, C, rows, HD), jnp.bfloat16),
-                    pltpu.VMEM((near, rows, HD), jnp.bfloat16),
-                    pltpu.VMEM((kept, S, C, 3, tl, HD), jnp.bfloat16),
-                    pltpu.VMEM((heads * groups, tl, HD), jnp.bfloat16),
-                    pltpu.SMEM((heads * groups,), jnp.int32),
-                    dma((near, S, C)),
-                    dma((near, S, C)),
-                    dma((2, near, S, C)),
-                    dma((heads * groups,)),
-                    dma((2, near, n)),
-                    dma((2, near, C)),
-                    dma((2, near, n)),
-                    dma((near, max(S - 1, 1))),
-                    dma((heads, S, C - 1)),
-                    dma((kept, S, C)),
-                    dma((kept, S, C)),
-                ],
-                compiler_params=pltpu.CompilerParams(
-                    collective_id=number, has_side_effects=True, vmem_limit_bytes=40 * 2**20
-                ),
-                name=f"guided_attention_{number}",
-            )(ordered, timestep, windows, segments)
-
-        return call
-
-    operands = (ordered, timestep, windows, segments)
-    if wide and tl * frames_here == rows:
-        out = lax.cond(fits[0] > 0, run(wide, near, short, 1), run(heads, heads, 0, 0), *operands)
+    heads_all = heads * groups
+
+    def general(x, timestep, windows, segments):
+        ordered, _ = pl.pallas_call(
+            functools.partial(gather_kernel, heads_all, W_MAX, (heads_all,) * W_MAX),
+            out_shape=(
+                jax.ShapeDtypeStruct((heads_all, 3, tl, HD), x.dtype),
+                jax.ShapeDtypeStruct((1,), jnp.int32),
+            ),
+            in_specs=[pl.BlockSpec(memory_space=pl.ANY), pl.BlockSpec(memory_space=pltpu.SMEM)],
+            out_specs=(
+                pl.BlockSpec(memory_space=pltpu.VMEM),
+                pl.BlockSpec(memory_space=pltpu.SMEM),
+            ),
+            scratch_shapes=[dma],
+            name="order_heads",
+            compiler_params=pltpu.CompilerParams(vmem_limit_bytes=56 * 2**20),
+        )(x, windows)
+        kept, near = 1, heads
+        return pl.pallas_call(
+            functools.partial(kernel, (S, C, F, heads, tl, frames_here, heads, heads, 0)),
+            out_shape=jax.ShapeDtypeStruct((heads, tl, S * HD), jnp.bfloat16),
+            in_specs=[pl.BlockSpec(memory_space=pl.ANY)]
+            + [pl.BlockSpec(memory_space=pltpu.SMEM)] * 3,
+            out_specs=pl.BlockSpec(memory_space=pltpu.VMEM),
+            scratch_shapes=[
+                pltpu.VMEM((near, C, 2, 3 * rows, HD), jnp.bfloat16),
+                pltpu.VMEM((near, C, rows, HD), jnp.bfloat16),
+                pltpu.VMEM((near, rows, HD), jnp.bfloat16),
+                pltpu.VMEM((kept, S, C, 3, tl, HD), jnp.bfloat16),
+                pltpu.VMEM((heads_all, tl, HD), jnp.bfloat16),
+                pltpu.SMEM((heads_all,), jnp.int32),
+                dma((near, S, C)),
+                dma((near, S, C)),
+                dma((2, near, S, C)),
+                dma((heads_all,)),
+                dma((2, near, n)),
+                dma((2, near, C)),
+                dma((2, near, n)),
+                dma((near, max(S - 1, 1))),
+                dma((heads, S, C - 1)),
+                dma((kept, S, C)),
+                dma((kept, S, C)),
+            ],
+            compiler_params=pltpu.CompilerParams(
+                collective_id=0, has_side_effects=True, vmem_limit_bytes=40 * 2**20
+            ),
+            name="guided_attention_0",
+        )(ordered, timestep, windows, segments)
+
+    if S == C == frames_here == 2 and tl % 128 == 0 and heads_all >= 8:
+        wide, near = heads_all // 3, 2 * heads_all // 3
+        plan, fits = pl.pallas_call(
+            functools.partial(plan_kernel, heads_all, W_MAX, (near, wide)),
+            out_shape=(
+                jax.ShapeDtypeStruct((2 * heads_all + W_MAX,), jnp.int32),
+                jax.ShapeDtypeStruct((1,), jnp.int32),
+            ),
+            in_specs=[pl.BlockSpec(memory_space=pltpu.SMEM)],
+            out_specs=(pl.BlockSpec(memory_space=pltpu.SMEM),) * 2,
+            name="plan_heads",
+        )(windows)
+
+        def fast(x, plan, timestep, windows, segments):
+            return fast_call(F, heads_all, wide, near, tl, 1)(x, plan, timestep, segments)
+
+        def slow(x, plan, timestep, windows, segments):
+            return general(x, timestep, windows, segments)
+
+        out = lax.cond(fits[0] > 0, fast, slow, x, plan, timestep, windows, segments)
     else:
-        out = run(heads, heads, 0, 0)(*operands)
+        out = general(x, timestep, windows, segments)
     return jnp.transpose(out, (1, 0, 2))
 
 

time: 78.4 us -> 83.5 us (1.065)
  Pallas kernels: 75.9 us -> 80.7 us
    pallas_call x2, Pallas kernels: 75.9 us -> 80.7 us  [the longest x1 78.5 us: fast(): fast_call(F, heads_all, wide, near, tl, 1)(x, plan, timestep, segments)]
where the time goes in v1:
time: 83.5 us; the launch traced here: 82.9 us
  Pallas kernels  80.7 us (97%)
  local copies, waits for them, and re-layouts  1.55 us (2%)
    pallas_call x1, Pallas kernels, fast(): fast_call(F, heads_all, wide, near, tl, 1)(x, plan, timestep, segments)  78.5 us
    pallas_call x1, Pallas kernels, body(): pl.pallas_call(functools.partial(plan_kernel, heads_all, W_MAX, (near, wi...  2.16 us

profile of v1, /device:TPU:0, one launch (start us, length us, event | category | flops | bytes accessed | tf_op | source)
XLA Modules:
  0.0 82.9 jit_solution(16439041826688860654)
XLA Ops:
  0.0 2.2 %plan_heads.1 = (s32[66]{0:T(128)S(1)}, s32[1]{0:T(128)}) custom-call(s32[32]{0:T(128)} %win_ref.1), custom_call_target="tpu_custom_call" | custom-call | tf_op jit(solution)/shard_map/plan_heads/pallas_call | solution.py:1015
  2.8 78.5 %conditional.1 = (bf16[8,256,256]{2,1,0:T(8,128)(2,1)S(1)}) conditional(s32[]{:T(128)} %bitcast, (bf16[3,256,4096]{2,1,0:T(8,128)(2,1)}, s32[32]{0:T(128)}, s32[1]{0:T(128)}, s32[8]{0:T(128)}) %tuple.15, (bf16[3,256,4096]{2,1,0:T(8,128)(2,1)}, s32[66]{0:T(128)S(1)}, s32[1]{0:T(128)}, s32[8]{0:T(128)}) %tuple.16), branch_computations={%region_0.0_spmd, %region_1.0_spmd} | conditional | bytes 25166556 | solution.py:1032
  2.8 78.5 %visiting_attention_1.1 = bf16[8,256,256]{2,1,0:T(8,128)(2,1)S(1)} custom-call(bf16[3,256,4096]{2,1,0:T(8,128)(2,1)} %get-tuple-element.29.x_ref, s32[66]{0:T(128)S(1)} %get-tuple-element.30.plan_ref, s32[1]{0:T(128)} %get-tuple-element.31.time_ref, s32[8]{0:T(128)} %get-tuple-element.32.seg_ref), custom_call_target="tpu_custom_call" | custom-call | tf_op jit(solution)/shard_map/cond/branch_1_fun/visiting_attention_1/pallas_call | solution.py:1027
  81.3 1.6 %copy.7 = bf16[8,256,256]{2,0,1:T(8,128)(2,1)} copy(bf16[8,256,256]{2,1,0:T(8,128)(2,1)S(1)} %get-tuple-element.37) | data formatting | bytes 2097152 | tf_op jit(solution)/shard_map/cond | solution.py:1032

commit v2 on v1

--- a/solution.py
+++ b/solution.py
@@ -13,8 +13,9 @@
 NEG = -1e30
 LOG2E = 1.4426950408889634
 MESH = pl.DeviceIdType.MESH
-KV_EARLY = 2
-KV_EVERY = 4
+DZ_EARLY, BACK_EARLY = 1, 2
+HOST_LAG, JOIN_LAG, HOME_LAG, DONE_LAG = 2, 3, 5, 6
+NEAR_HOME_LAG, NEAR_DONE_LAG = 2, 3
 
 
 def gather_kernel(heads_all, levels, room, x_ref, win_ref, out_ref, fits_ref, sem):
@@ -424,27 +425,24 @@
 
 
 def plan_kernel(heads_all, levels, room, win_ref, plan_ref, fits_ref):
-    def place(level):
-        def step(head, slot):
-            hit = win_ref[head] == level
-
-            @pl.when(hit)
-            def _():
-                plan_ref[slot] = head
-                plan_ref[heads_all + head] = slot
-
-            return slot + hit.astype(jnp.int32)
-
-        return step
-
-    slot = jnp.int32(0)
+    many = [jnp.int32(0)] * (levels + 2)
+    for head in range(heads_all):
+        for level in range(1, levels + 1):
+            many[level] = many[level] + (win_ref[head] >= level).astype(jnp.int32)
     fits = jnp.int32(1)
-    for level in range(levels, -1, -1):
-        slot = lax.fori_loop(0, heads_all, place(level), slot)
-        if level:
-            plan_ref[2 * heads_all + level - 1] = slot
-            fits = fits * (slot <= room[level - 1]).astype(jnp.int32)
+    for level in range(1, levels + 1):
+        plan_ref[2 * heads_all + level - 1] = many[level]
+        fits = fits * (many[level] <= room[level - 1]).astype(jnp.int32)
     fits_ref[0] = fits
+    place = [many[level + 1] for level in range(levels + 1)]
+    for head in range(heads_all):
+        slot = place[0]
+        for level in range(1, levels + 1):
+            slot = jnp.where(win_ref[head] == level, place[level], slot)
+        for level in range(levels + 1):
+            place[level] = place[level] + (win_ref[head] == level).astype(jnp.int32)
+        plan_ref[slot] = head
+        plan_ref[heads_all + head] = slot
 
 
 def fast_kernel(
@@ -470,6 +468,16 @@
     lanes = [slice(128 * j, 128 * (j + 1)) for j in range(tl // 128)]
     k = len(lanes)
 
+    barrier = pltpu.get_barrier_semaphore()
+    for axis, other in (("seq", 1 - s), ("cfg", 1 - c)):
+        pl.semaphore_signal(barrier, inc=1, device_id={axis: other}, device_id_type=MESH)
+    for ok, step in ((up_ok, 1), (down_ok, -1)):
+        @pl.when(ok)
+        def _():
+            pl.semaphore_signal(
+                barrier, inc=1, device_id={"frame": f + step}, device_id_type=MESH
+            )
+
     own = (xq, xk, xv)
     for part, ref in enumerate(own):
         @pl.loop(0, heads_all)
@@ -482,16 +490,6 @@
     def loaded(part):
         pltpu.make_async_copy(own[part], own[part], load_sem.at[part]).wait()
 
-    barrier = pltpu.get_barrier_semaphore()
-    for axis, other in (("seq", 1 - s), ("cfg", 1 - c)):
-        pl.semaphore_signal(barrier, inc=1, device_id={axis: other}, device_id_type=MESH)
-    for ok, step in ((up_ok, 1), (down_ok, -1)):
-        @pl.when(ok)
-        def _():
-            pl.semaphore_signal(
-                barrier, inc=1, device_id={"frame": f + step}, device_id_type=MESH
-            )
-
     def remote(src, dst, send, arrive, where):
         return pltpu.make_async_remote_copy(
             src_ref=src, dst_ref=dst, send_sem=send, recv_sem=arrive,
@@ -626,15 +624,17 @@
         for part in range(2):
             kw[i, part, pl.ds(tl, tl), :] = own[1 + part][plan_ref[i]]
 
-    def spread_kv(i):
+    first_kv = [jnp.where(s == side, DZ_EARLY, BACK_EARLY) for side in range(2)]
+
+    def spread_kv(early):
         for side, ok in ((0, up_ok), (1, down_ok)):
             @pl.when(ok)
             def _():
-                send_kv(side, i).start()
-
-    EARLY = min(W, KV_EARLY)
-    for i in range(EARLY):
-        spread_kv(i)
+                @pl.loop(0 if early else first_kv[side], first_kv[side] if early else W)
+                def _(i):
+                    send_kv(side, i).start()
+
+    spread_kv(True)
 
     for ok, start in ((down_ok, 0), (up_ok, 2 * tl)):
         @pl.when(jnp.logical_not(ok))
@@ -692,12 +692,6 @@
             for copy in send_third(m):
                 copy.start()
 
-        late = EARLY + n // KV_EVERY
-
-        @pl.when((lax.rem(n, KV_EVERY) == KV_EVERY - 1) & (late < W))
-        def _():
-            spread_kv(late)
-
         @pl.when(n < L)
         def _():
             here = plan_ref[M + n]
@@ -705,11 +699,7 @@
             la[n] = out.astype(jnp.bfloat16)
             send_local(n).start()
 
-    spread = min(W, EARLY + max(N + LAG, L) // KV_EVERY)
-
-    @pl.loop(spread, W)
-    def _(i):
-        spread_kv(i)
+    spread_kv(False)
 
     def weigh(i, home, parts):
         tops = [
@@ -783,7 +773,7 @@
     first_keys = pl.multiple_of(tl * (1 - s), tl)
     per = -(-N // W)
 
-    @pl.loop(0, W + 4)
+    @pl.loop(0, W + DONE_LAG)
     def _(j):
         @pl.when(j < W)
         def _():
@@ -820,9 +810,9 @@
             ov[j] = out
             keep_stats(vs, j, top, total)
 
-        @pl.when((j >= 2) & (j < W + 2))
-        def _():
-            m = j - 2
+        @pl.when((j >= HOST_LAG) & (j < W + HOST_LAG))
+        def _():
+            m = j - HOST_LAG
             send_stats(m).wait_recv()
             (share,) = weigh(m, hr, [(vs, m, reach(1, m) & (same_visit | same_beyond))])
             ov[m] = share * ov[m]
@@ -835,30 +825,30 @@
             def _():
                 join(W + n)
 
-            late = per * (j - 3) + part
+            late = per * (j - NEAR_HOME_LAG) + part
 
             @pl.when((late >= 0) & (late < N))
             def _():
                 weigh_home(W + late)
 
-        @pl.when((j >= 2) & (j < W + 2))
-        def _():
-            join(j - 2)
-
-        @pl.when(j >= 4)
-        def _():
-            weigh_home(j - 4)
+        @pl.when((j >= JOIN_LAG) & (j < W + JOIN_LAG))
+        def _():
+            join(j - JOIN_LAG)
+
+        @pl.when((j >= HOME_LAG) & (j < W + HOME_LAG))
+        def _():
+            weigh_home(j - HOME_LAG)
 
         for part in range(per):
-            late = per * (j - 3) + part
+            late = per * (j - NEAR_DONE_LAG) + part
 
             @pl.when((late >= 0) & (late < N))
             def _():
                 finish(W + late)
 
-        @pl.when(j >= 4)
-        def _():
-            finish(j - 4)
+        @pl.when(j >= DONE_LAG)
+        def _():
+            finish(j - DONE_LAG)
 
     @pl.loop(0, M)
     def _(i):

time: 83.5 us -> 73 us (0.87)
  Pallas kernels: 80.7 us -> 70.6 us
    pallas_call x1, Pallas kernels: 78.5 us -> 69.1 us  [fast(): fast_call(F, heads_all, wide, near, tl, 1)(x, plan, timestep, segments)]
where the time goes in v2:
time: 73 us; the launch traced here: 72.8 us
  Pallas kernels  70.6 us (97%)
  local copies, waits for them, and re-layouts  1.55 us (2%)
    pallas_call x1, Pallas kernels, fast(): fast_call(F, heads_all, wide, near, tl, 1)(x, plan, timestep, segments)  69.1 us
    cond x1, local copies, waits for them, and re-layouts, body(): lax.cond(fits[0] > 0, fast, slow, x, plan, timestep, windows, segments)  1.55 us
    pallas_call x1, Pallas kernels, body(): pl.pallas_call(functools.partial(plan_kernel, heads_all, W_MAX, (near, wi...  1.51 us

profile of v2, /device:TPU:0, one launch (start us, length us, event | category | flops | bytes accessed | tf_op | source)
XLA Modules:
  0.0 72.8 jit_solution(16808596146730178797)
XLA Ops:
  0.0 1.5 %plan_heads.1 = (s32[66]{0:T(128)S(1)}, s32[1]{0:T(128)}) custom-call(s32[32]{0:T(128)} %win_ref.1), custom_call_target="tpu_custom_call" | custom-call | tf_op jit(solution)/shard_map/plan_heads/pallas_call | solution.py:1005
  2.2 69.1 %conditional.1 = (bf16[8,256,256]{2,1,0:T(8,128)(2,1)S(1)}) conditional(s32[]{:T(128)} %bitcast, (bf16[3,256,4096]{2,1,0:T(8,128)(2,1)}, s32[32]{0:T(128)}, s32[1]{0:T(128)}, s32[8]{0:T(128)}) %tuple.15, (bf16[3,256,4096]{2,1,0:T(8,128)(2,1)}, s32[66]{0:T(128)S(1)}, s32[1]{0:T(128)}, s32[8]{0:T(128)}) %tuple.16), branch_computations={%region_0.0_spmd, %region_1.0_spmd} | conditional | bytes 25166556 | solution.py:1022
  2.2 69.1 %visiting_attention_1.1 = bf16[8,256,256]{2,1,0:T(8,128)(2,1)S(1)} custom-call(bf16[3,256,4096]{2,1,0:T(8,128)(2,1)} %get-tuple-element.29.x_ref, s32[66]{0:T(128)S(1)} %get-tuple-element.30.plan_ref, s32[1]{0:T(128)} %get-tuple-element.31.time_ref, s32[8]{0:T(128)} %get-tuple-element.32.seg_ref), custom_call_target="tpu_custom_call" | custom-call | tf_op jit(solution)/shard_map/cond/branch_1_fun/visiting_attention_1/pallas_call | solution.py:1017
  71.3 1.6 %copy.7 = bf16[8,256,256]{2,0,1:T(8,128)(2,1)} copy(bf16[8,256,256]{2,1,0:T(8,128)(2,1)S(1)} %get-tuple-element.37) | data formatting | bytes 2097152 | tf_op jit(solution)/shard_map/cond | solution.py:1022

commit v3 on v2

--- a/solution.py
+++ b/solution.py
@@ -13,7 +13,7 @@
 NEG = -1e30
 LOG2E = 1.4426950408889634
 MESH = pl.DeviceIdType.MESH
-DZ_EARLY, BACK_EARLY = 1, 2
+DZ_EARLY, BACK_EARLY = 2, 3
 HOST_LAG, JOIN_LAG, HOME_LAG, DONE_LAG = 2, 3, 5, 6
 NEAR_HOME_LAG, NEAR_DONE_LAG = 2, 3
 
@@ -624,7 +624,7 @@
         for part in range(2):
             kw[i, part, pl.ds(tl, tl), :] = own[1 + part][plan_ref[i]]
 
-    first_kv = [jnp.where(s == side, DZ_EARLY, BACK_EARLY) for side in range(2)]
+    first_kv = [jnp.where(s == side, min(DZ_EARLY, W), min(BACK_EARLY, W)) for side in range(2)]
 
     def spread_kv(early):
         for side, ok in ((0, up_ok), (1, down_ok)):

time: 73 us -> 70.9 us (0.971)
  Pallas kernels: 70.6 us -> 68.4 us
    pallas_call x1, Pallas kernels: 69.1 us -> 66.9 us  [fast(): fast_call(F, heads_all, wide, near, tl, 1)(x, plan, timestep, segments)]
where the time goes in v3:
time: 70.9 us; the launch traced here: 70.7 us
  Pallas kernels  68.4 us (96%)
  local copies, waits for them, and re-layouts  1.55 us (2%)
    pallas_call x1, Pallas kernels, fast(): fast_call(F, heads_all, wide, near, tl, 1)(x, plan, timestep, segments)  66.9 us
    cond x1, local copies, waits for them, and re-layouts, body(): lax.cond(fits[0] > 0, fast, slow, x, plan, timestep, windows, segments)  1.55 us
    pallas_call x1, Pallas kernels, body(): pl.pallas_call(functools.partial(plan_kernel, heads_all, W_MAX, (near, wi...  1.51 us

profile of v3, /device:TPU:0, one launch (start us, length us, event | category | flops | bytes accessed | tf_op | source)
XLA Modules:
  0.0 70.7 jit_solution(8306334271519592947)
XLA Ops:
  0.0 1.5 %plan_heads.1 = (s32[66]{0:T(128)S(1)}, s32[1]{0:T(128)}) custom-call(s32[32]{0:T(128)} %win_ref.1), custom_call_target="tpu_custom_call" | custom-call | tf_op jit(solution)/shard_map/plan_heads/pallas_call | solution.py:1005
  2.2 66.9 %conditional.1 = (bf16[8,256,256]{2,1,0:T(8,128)(2,1)S(1)}) conditional(s32[]{:T(128)} %bitcast, (bf16[3,256,4096]{2,1,0:T(8,128)(2,1)}, s32[32]{0:T(128)}, s32[1]{0:T(128)}, s32[8]{0:T(128)}) %tuple.15, (bf16[3,256,4096]{2,1,0:T(8,128)(2,1)}, s32[66]{0:T(128)S(1)}, s32[1]{0:T(128)}, s32[8]{0:T(128)}) %tuple.16), branch_computations={%region_0.0_spmd, %region_1.0_spmd} | conditional | bytes 25166556 | solution.py:1022
  2.2 66.9 %visiting_attention_1.1 = bf16[8,256,256]{2,1,0:T(8,128)(2,1)S(1)} custom-call(bf16[3,256,4096]{2,1,0:T(8,128)(2,1)} %get-tuple-element.29.x_ref, s32[66]{0:T(128)S(1)} %get-tuple-element.30.plan_ref, s32[1]{0:T(128)} %get-tuple-element.31.time_ref, s32[8]{0:T(128)} %get-tuple-element.32.seg_ref), custom_call_target="tpu_custom_call" | custom-call | tf_op jit(solution)/shard_map/cond/branch_1_fun/visiting_attention_1/pallas_call | solution.py:1017
  69.1 1.6 %copy.7 = bf16[8,256,256]{2,0,1:T(8,128)(2,1)} copy(bf16[8,256,256]{2,1,0:T(8,128)(2,1)S(1)} %get-tuple-element.37) | data formatting | bytes 2097152 | tf_op jit(solution)/shard_map/cond | solution.py:1022
